TPU v7x, 32 devices: a whole 2x2x4 slice. The times are simulated.
32 devices in a mesh: groups: 2 (over y), row: 16 (over z, x, core).
Axes of the slice: x: 2, y: 2, z: 4, core: 2. Of those that a mesh axis runs over, the one named last changes fastest.
Arguments:
- homolog_activation: float32 [32, 512, 256], P('groups', 'row'), parts along dimension 0, may hold values from -6 to 6
- homolog_entry_valid: int32 [32, 512], P('groups', 'row'), parts along dimension 0, may hold values 0 or 1
- amino_valid_flags: int32 [1024], P(('groups', 'row')), parts along dimension 0, may hold values 0 or 1
- first_factor_weights: float32 [256, 32], replicated, may hold values from -0.375 to 0.375
- second_factor_weights: float32 [256, 32], replicated, may hold values from -0.375 to 0.375
- final_linear_weights: float32 [1024, 128], replicated, may hold values from -0.1875 to 0.1875
- couple_delta_deriv: float32 [1024, 512, 128], P(('groups', 'row')), parts along dimension 0, may hold values from -6 to 6
Outputs:
- alignment_grad: float32 [32, 512, 256], P('groups', 'row'), parts along dimension 0
- left_weight_grad: float32 [512, 32], P('groups'), parts along dimension 0
- right_weight_grad: float32 [512, 32], P('groups'), parts along dimension 0
- out_weight_grad: float32 [2048, 128], P('groups'), parts along dimension 0
There are 2 independent parts, one for each index of `groups`. A program takes and returns all parts, laid end to end along the dimension named above; an argument that names none is the same for every part. Nothing has to cross between parts.
All inputs are finite; a program needn't handle non-finite values. No bound on the sum of `homolog_entry_valid` or of `amino_valid_flags` on one device may be relied on, other than what follows from the above.
Results may differ from a plain program's by a relative error of at most 0.0003.
Values sent between devices are 32-bit elements; how exact they have to be, the bound alone decides.
A program may use at most 128 MiB of HBM per device.

v0:
```python
import functools

import jax
import jax.numpy as jnp
from jax import lax
from jax.experimental import pallas as pl
from jax.experimental.pallas import tpu as pltpu
from jax.sharding import PartitionSpec as P

F32, BF16 = jnp.float32, jnp.bfloat16
LANES = 128


def split(x):
    hi = x.astype(BF16)
    return hi, (x - hi.astype(F32)).astype(BF16)


def nn(a, b):
    return jnp.dot(a, b, preferred_element_type=F32)


def nt(a, b):
    return lax.dot_general(a, b, (((1,), (1,)), ((), ())), preferred_element_type=F32)


def remote(src, dst, send, recv, target):
    return pltpu.make_async_remote_copy(
        src_ref=src,
        dst_ref=dst,
        send_sem=send,
        recv_sem=recv,
        device_id={"row": target},
        device_id_type=pl.DeviceIdType.MESH,
    )


def each(start, stop, body):
    def one(k, _):
        body(k)
        return 0

    lax.fori_loop(start, stop, one, 0)


def sides(n):
    half, across = n // 2, 1
    while half % (2 * across) == 0 and 4 * across * across <= half:
        across *= 2
    return half // across, across


class Place:
    def __init__(self, n):
        self.n = n
        self.deep, self.wide = sides(n)
        self.me = lax.axis_index("row")
        self.core = lax.rem(self.me, 2)
        chip = lax.div(self.me, 2)
        self.x = lax.rem(chip, self.wide)
        self.z = lax.div(chip, self.wide)
        self.partner = self.at(0, 0, True)

    def at(self, k, m, other=False):
        z = lax.rem(self.z + k + self.deep, self.deep)
        x = lax.rem(self.x + m + self.wide, self.wide)
        core = 1 - self.core if other else self.core
        return (z * self.wide + x) * 2 + core

    def signal(self):
        barrier = pltpu.get_barrier_semaphore()

        def tell(target):
            pl.semaphore_signal(barrier, inc=1, device_id={"row": target}, device_id_type=pl.DeviceIdType.MESH)

        tell(self.partner)
        each(1, self.wide, lambda m: tell(self.at(0, m)))
        each(1, self.deep, lambda k: tell(self.at(k, 0)))

    def wait(self):
        pl.semaphore_wait(pltpu.get_barrier_semaphore(), self.deep + self.wide - 1)


class Gather:
    def __init__(self, place, own, out, z_send, x_send, c_send, recv):
        self.p, self.own, self.out = place, own, out
        self.z_send, self.x_send, self.c_send, self.recv = z_send, x_send, c_send, recv

    def copy(self, src, owner, send, target):
        return remote(src, self.out(owner), send, self.recv.at[owner], target)

    def start(self):
        p = self.p
        each(1, p.deep, lambda k: self.copy(self.own, p.me, self.z_send.at[k], p.at(k, 0)).start())
        each(1, p.wide, lambda m: self.copy(self.own, p.me, self.x_send.at[m], p.at(0, m)).start())
        self.copy(self.own, p.me, self.c_send.at[0], p.partner).start()

    def landed(self, owner):
        self.copy(self.out(owner), owner, self.z_send.at[0], self.p.partner).wait_recv()

    def cross(self):
        p = self.p

        def one(k):
            owner = p.at(-k, 0)
            self.landed(owner)
            block = self.out(owner)
            each(1, p.wide, lambda m: self.copy(block, owner, self.x_send.at[k * p.wide + m], p.at(0, m)).start())
            self.copy(block, owner, self.c_send.at[k * p.wide], p.partner).start()

        each(1, p.deep, one)

    def pair(self):
        p = self.p

        def one(k):
            def two(m):
                owner = p.at(-k, -m)
                self.landed(owner)
                self.copy(self.out(owner), owner, self.c_send.at[k * p.wide + m], p.partner).start()

            each(1, p.wide, two)

        each(0, p.deep, one)

    def finish(self):
        p = self.p
        each(0, p.deep, lambda k: each(0, p.wide, lambda m: self.landed(p.at(-k, -m, True))))

        def sent(sem):
            self.copy(self.own, p.me, sem, p.partner).wait_send()

        each(1, p.deep, lambda k: sent(self.z_send.at[k]))
        each(0, p.deep, lambda k: each(1, p.wide, lambda m: sent(self.x_send.at[k * p.wide + m])))
        each(0, p.deep * p.wide, lambda i: sent(self.c_send.at[i]))


class Scatter:
    def __init__(self, place, x, near, mid, far, staged, *sems):
        self.p, self.x, self.near, self.mid, self.far, self.staged = place, x, near, mid, far, staged
        self.near_send, self.near_recv, self.mid_send, self.mid_recv, self.far_send, self.far_recv = sems

    def near_copy(self, k, m):
        p, i = self.p, k * self.p.wide + m
        return remote(
            self.x(p.at(k, m, True)), self.near.at[i], self.near_send.at[i], self.near_recv.at[i], p.partner
        )

    def mid_copy(self, k, m):
        p, i = self.p, k * self.p.wide + m
        return remote(self.staged.at[i], self.mid.at[i], self.mid_send.at[i], self.mid_recv.at[i], p.at(0, m))

    def far_copy(self, k):
        p = self.p
        return remote(
            self.staged.at[k * p.wide], self.far.at[k], self.far_send.at[k], self.far_recv.at[k], p.at(k, 0)
        )

    def over(self, first, body):
        p = self.p
        each(0, p.deep, lambda k: each(first, p.wide, lambda m: body(k, m)))

    def start(self):
        self.over(1, lambda k, m: self.near_copy(k, m).start())
        each(0, self.p.deep, lambda k: self.near_copy(k, 0).start())

    def pair(self):
        p = self.p

        def merge(k, m):
            i = k * p.wide + m
            self.near_copy(k, m).wait_recv()
            self.staged[i] = self.x(p.at(k, m))[...] + self.near[i]

        def pass_on(k, m):
            merge(k, m)
            self.mid_copy(k, m).start()

        self.over(1, pass_on)
        each(0, p.deep, lambda k: merge(k, 0))

    def cross(self):
        p = self.p

        def merge(k):
            i = k * p.wide

            def one(m):
                self.mid_copy(k, m).wait_recv()
                self.staged[i] = self.staged[i] + self.mid[i + m]

            each(1, p.wide, one)

        def pass_on(k):
            merge(k)
            self.far_copy(k).start()

        each(1, p.deep, pass_on)
        merge(0)

    def finish(self):
        def one(k):
            self.far_copy(k).wait_recv()
            self.staged[0] = self.staged[0] + self.far[k]

        each(1, self.p.deep, one)
        self.over(0, lambda k, m: self.near_copy(k, m).wait_send())
        self.over(1, lambda k, m: self.mid_copy(k, m).wait_send())
        each(1, self.p.deep, lambda k: self.far_copy(k).wait_send())


def gather_sems(n):
    deep, wide = sides(n)
    return [pltpu.SemaphoreType.DMA((c,)) for c in (deep, deep * wide, deep * wide, n)]


def scatter_scratch(n, block):
    deep, wide = sides(n)
    most = deep * wide
    return [pltpu.VMEM((c,) + block, F32) for c in (most, most, deep, most)] + [
        pltpu.SemaphoreType.DMA((c,)) for c in (most, most, most, most, deep, deep)
    ]


def three(dot, a, b):
    a_hi, a_lo = split(a)
    b_hi, b_lo = split(b)
    return dot(a_hi, b_hi) + dot(a_hi, b_lo) + dot(a_lo, b_hi)


def kernel(
    n,
    step,
    fam,
    act,
    valid,
    flags,
    w_left,
    w_right,
    w_final,
    cdd_hbm,
    align,
    total_sum,
    *scratch,
):
    scratch = list(scratch)

    def take(count):
        taken = scratch[:count]
        del scratch[:count]
        return taken

    cdd, u, s_hi, s_lo, c_hi, c_lo, terms, terms_split = take(8)
    left, own_right, marks_all, right_all, flat_marks, turned, rt_hi, rt_lo, left_grad, both, packed = take(11)
    board, marks, keep_rows, present_row = take(4)
    (load,) = take(1)
    mark_sems, right_sems, sum_sems = take(4), take(4), take(4)
    right_scatter, sum_scatter = take(10), take(10)
    assert not scratch

    rows, total, pair = cdd.shape
    width = w_left.shape[0]
    groups = rows // step
    piece = packed.shape[0] // n
    place = Place(n)
    place.signal()

    def fetch(g):
        at = pl.ds(g * step, step)
        return pltpu.make_async_copy(cdd_hbm.at[at], cdd.at[at], load.at[g])

    each(0, groups, lambda g: fetch(g).start())

    board[...] = jnp.zeros_like(board)
    board[:fam, :rows] = valid[...].astype(F32)
    board[fam : fam + 1, :rows] = flags[...].astype(F32)
    marks[...] = board[...].T[:rows]
    keep_t = marks[:, :fam]
    lane = lax.broadcasted_iota(jnp.int32, (rows, LANES), 1)
    kept = jnp.where(lane < fam, marks[...], 0.0)
    for g in range(groups):
        keep_rows[g] = kept[g * step : (g + 1) * step]
        present_row[g] = board[fam : fam + 1, g * step : (g + 1) * step]

    w_cat = jnp.concatenate([w_left[...], w_right[...]], axis=0)
    projected = three(nt, act[...], w_cat)
    rights = []
    for s in range(fam):
        one = projected[s * rows : (s + 1) * rows] * keep_t[:, s : s + 1]
        rights.append(one[:, width:])
        left[pl.ds(s, rows, stride=fam), :] = jnp.concatenate([one, jnp.zeros((rows, LANES - 2 * width), F32)], axis=1)
    own_right[...] = jnp.concatenate(rights, axis=1)

    mark_gather = Gather(place, marks, lambda o: marks_all.at[o], *mark_sems)
    right_gather = Gather(place, own_right, lambda o: right_all.at[o], *right_sems)
    place.wait()
    mark_gather.start()
    right_gather.start()
    marks_all[place.me] = marks[...]
    right_all[place.me] = own_right[...]

    def weights(q):
        parts = [w_final[pl.ds(2 * q + b, width, stride=width), :] for b in range(2)]
        return jnp.concatenate(parts, axis=1)

    l_hi, l_lo = split(left[:, :width])
    l_three = jnp.concatenate([l_hi.astype(F32), l_hi.astype(F32), l_lo.astype(F32)], axis=1).astype(BF16)

    def make_u(q):
        w_hi, w_lo = split(weights(q))
        value = nn(l_three, jnp.concatenate([w_hi, w_lo, w_hi], axis=0))
        for b in range(2):
            for r in range(rows):
                u[r, pl.ds(2 * q + b, fam, stride=width), :] = value[
                    r * fam : (r + 1) * fam, b * pair : (b + 1) * pair
                ]

    each(0, width // 4, make_u)
    mark_gather.cross()
    each(width // 4, width // 2, make_u)
    mark_gather.pair()
    right_gather.cross()
    terms[...] = jnp.zeros_like(terms)
    mark_gather.finish()
    for o in range(n):
        flat_marks[o * rows : (o + 1) * rows, :] = marks_all[o]

    def lanes_of(g):
        return pl.ds(pl.multiple_of(g * step * pair, step * pair), step * pair)

    def make_terms(g):
        fetch(g).wait()
        count = nt(flat_marks[...].astype(BF16), keep_rows[g].astype(BF16))
        factor = flat_marks[:, fam : fam + 1] * present_row[g] / jnp.maximum(count, 1.0)
        hi, lo = split(jnp.concatenate([cdd[g * step + q] * factor[:, q : q + 1] for q in range(step)], axis=1))
        lanes = lanes_of(g)
        s_hi[:, lanes] = hi
        s_lo[:, lanes] = lo
        u_hi, u_lo = split(jnp.concatenate([u[g * step + q] for q in range(step)], axis=1))
        terms[...] += nt(hi, u_hi) + nt(hi, u_lo) + nt(lo, u_hi)

    each(0, groups // 4, make_terms)
    right_gather.pair()
    each(groups // 4, groups, make_terms)
    right_gather.finish()

    for o in range(n):
        terms_split[o] = terms[o * rows : (o + 1) * rows, :]
    right_sum = Scatter(place, lambda o: terms_split.at[o], *right_scatter)
    right_sum.start()
    for o in range(n):
        terms[o * rows : (o + 1) * rows, :] = right_all[o]
    for t in range(total // LANES):
        at = slice(t * LANES, (t + 1) * LANES)
        turned[t] = terms[at, :].T
        for c in range(width):
            hi, lo = split(turned[t, pl.ds(c, fam, stride=width), :])
            rt_hi[c * fam : (c + 1) * fam, at] = hi
            rt_lo[c * fam : (c + 1) * fam, at] = lo

    def make_carried(g):
        lanes = lanes_of(g)
        hi, lo = split(
            nn(rt_hi[...], s_hi[:, lanes]) + nn(rt_hi[...], s_lo[:, lanes]) + nn(rt_lo[...], s_hi[:, lanes])
        )
        c_hi[:, lanes] = hi
        c_lo[:, lanes] = lo

    each(0, groups // 4, make_carried)
    right_sum.pair()
    each(groups // 4, 3 * groups // 4, make_carried)
    right_sum.cross()
    each(3 * groups // 4, groups, make_carried)

    t_hi, t_lo = split(left[...].T[:width])
    t_both = jnp.concatenate([t_hi, t_lo], axis=0)
    left_grad[...] = jnp.zeros_like(left_grad)

    def contract(q):
        def regroup(ref):
            cols = []
            for c in range(2):
                at = pl.ds(pl.multiple_of((2 * q + c) * fam, fam), fam)
                cols.append(jnp.concatenate([ref[at, r * pair : (r + 1) * pair] for r in range(rows)], axis=0))
            return jnp.concatenate(cols, axis=1)

        hi, lo = regroup(c_hi), regroup(c_lo)
        w_hi, w_lo = split(weights(q))
        left_grad[:, :width] += nt(hi, w_hi) + nt(hi, w_lo) + nt(lo, w_hi)
        two = nn(t_both, hi)
        value = two[:width] + two[width:] + nn(t_hi, lo)
        for c in range(2):
            at = pl.ds(pl.multiple_of((2 * q + c) * width, width), width)
            packed[at, :] = value[:, c * pair : (c + 1) * pair]

    each(0, width // 2, contract)
    right_sum.finish()

    mine = right_scatter[3]
    for s in range(fam):
        one = jnp.concatenate(
            [left_grad[pl.ds(s, rows, stride=fam), :][:, :width], mine[0, :, s * width : (s + 1) * width]], axis=1
        )
        both[s * rows : (s + 1) * rows, :] = jnp.concatenate(
            [one * keep_t[:, s : s + 1], jnp.zeros((rows, LANES - 2 * width), F32)], axis=1
        )
    grads = three(nn, both[...].T, act[...])[: 2 * width]
    base = width * width
    tiles = act.shape[1] // LANES
    for t in range(tiles):
        packed[base + t * 2 * width : base + (t + 1) * 2 * width, :] = grads[:, t * LANES : (t + 1) * LANES]
    end = base + tiles * 2 * width
    if end < packed.shape[0]:
        packed[end:, :] = jnp.zeros((packed.shape[0] - end, LANES), F32)

    def piece_of(ref):
        return lambda o: ref.at[pl.ds(pl.multiple_of(o * piece, 8), piece), :]

    weight_sum = Scatter(place, piece_of(packed), *sum_scatter)
    weight_sum.start()
    align[...] = three(nn, both[:, : 2 * width], w_cat)
    weight_sum.pair()
    weight_sum.cross()
    weight_sum.finish()
    summed = sum_scatter[3]
    spread = Gather(place, summed.at[0], piece_of(total_sum), *sum_sems)
    spread.start()
    total_sum[pl.ds(pl.multiple_of(place.me * piece, 8), piece), :] = summed[0]
    spread.cross()
    spread.pair()
    spread.finish()


def unpack_kernel(align, total_sum, align_out, left_w, right_w, out_w):
    width, depth = left_w.shape
    base = width * width
    align_out[...] = align[...]
    for c in range(width):
        out_w[pl.ds(c, width, stride=width), :] = total_sum[c * width : (c + 1) * width, :]
    for t in range(depth // LANES):
        at = slice(t * LANES, (t + 1) * LANES)
        first = base + t * 2 * width
        left_w[:, at] = total_sum[first : first + width, :]
        right_w[:, at] = total_sum[first + width : first + 2 * width, :]


def local(n, act, valid, flags, w_left, w_right, w_final, cdd):
    rows, total, pair = cdd.shape
    fam, _, depth = act.shape
    width = w_left.shape[1]
    feats = width * fam
    step = min(4, rows)
    used = width * width + 2 * depth * width // LANES
    piece = -(-used // (8 * n)) * 8
    vm = pl.BlockSpec(memory_space=pltpu.VMEM)
    f32 = lambda *shape: pltpu.VMEM(shape, F32)
    b16 = lambda *shape: pltpu.VMEM(shape, BF16)
    align, total_sum = pl.pallas_call(
        functools.partial(kernel, n, step, fam),
        out_shape=tuple(
            jax.ShapeDtypeStruct(shape, F32)
            for shape in ((fam * rows, depth), (n * piece, LANES))
        ),
        in_specs=[vm] * 6 + [pl.BlockSpec(memory_space=pl.ANY)],
        out_specs=(vm,) * 2,
        scratch_shapes=[
            f32(rows, total, pair),
            f32(rows, feats, pair),
            b16(total, rows * pair),
            b16(total, rows * pair),
            b16(feats, rows * pair),
            b16(feats, rows * pair),
            f32(total, feats),
            f32(n, rows, feats),
            f32(rows * fam, LANES),
            f32(rows, feats),
            f32(n, rows, LANES),
            f32(n, rows, feats),
            f32(total, LANES),
            f32(total // LANES, feats, LANES),
            b16(feats, total),
            b16(feats, total),
            f32(rows * fam, LANES),
            f32(fam * rows, LANES),
            f32(n * piece, LANES),
            f32(LANES, LANES),
            f32(rows, LANES),
            f32(rows // step, step, LANES),
            f32(rows // step, 1, step),
            pltpu.SemaphoreType.DMA((rows // step,)),
        ]
        + gather_sems(n) * 3
        + scatter_scratch(n, (rows, feats))
        + scatter_scratch(n, (piece, LANES)),
        name="outer_mean_grad",
        compiler_params=pltpu.CompilerParams(collective_id=0, has_side_effects=True, vmem_limit_bytes=60 << 20),
    )(
        act.reshape(fam * rows, depth),
        valid,
        flags.reshape(1, rows),
        w_left.T,
        w_right.T,
        w_final,
        cdd,
    )
    align, left_w, right_w, out_w = pl.pallas_call(
        unpack_kernel,
        out_shape=tuple(
            jax.ShapeDtypeStruct(shape, F32)
            for shape in ((fam * rows, depth), (width, depth), (width, depth), (width * width, pair))
        ),
        in_specs=[vm] * 2,
        out_specs=(vm,) * 4,
        name="unpack",
    )(align, total_sum)
    return align.reshape(fam, rows, depth), left_w.T, right_w.T, out_w


def solution(mesh):
    in_specs = (
        P("groups", "row", None),
        P("groups", "row"),
        P(("groups", "row")),
        P(),
        P(),
        P(),
        P(("groups", "row"), None, None),
    )
    out_specs = (P("groups", "row", None), P("groups", None), P("groups", None), P("groups", None))
    body = functools.partial(local, mesh.shape["row"])
    return jax.shard_map(body, mesh=mesh, in_specs=in_specs, out_specs=out_specs, check_vma=False)
```

profile of v0, /device:TPU:0, one launch (start us, length us, event | category | flops | bytes accessed | tf_op | source)
XLA Modules:
  0.0 73.9 jit_solution(16906232152647681818)
XLA Ops:
  0.6 70.8 %outer_mean_grad.1 = (f32[512,256]{1,0:T(8,128)}, f32[1152,128]{1,0:T(8,128)}) custom-call(f32[512,256]{1,0:T(8,128)} %bitcast.7, s32[16,32]{1,0:T(8,128)} %valid.1, s32[1,32]{1,0:T(1,128)} %bitcast.10, f32[32,256]{1,0:T(8,128)} %bitcast.8, f32[32,256]{1,0:T(8,128)} %bitcast.9, f32[1024,128]{1,0:T(8,128)} %w_final.1, f32[32,512,128]{2,1,0:T(8,128)} %cdd_hbm.1), custom_call_target="tpu_custom_call" | custom-call | tf_op jit(solution)/shard_map/outer_mean_grad/pallas_call | solution.py:458
  71.4 2.5 %unpack.1 = (f32[512,256]{1,0:T(8,128)}, f32[32,256]{1,0:T(8,128)}, f32[32,256]{1,0:T(8,128)}, f32[1024,128]{1,0:T(8,128)}) custom-call(f32[512,256]{1,0:T(8,128)} %get-tuple-element.10.align, f32[1152,128]{1,0:T(8,128)} %get-tuple-element.11.total_sum), custom_call_target="tpu_custom_call" | custom-call | tf_op jit(solution)/shard_map/unpack/pallas_call | solution.py:506
where the time goes:
time: 74.1 us; the launch traced here: 73.9 us
  Pallas kernels  73.3 us (99%)
    pallas_call x1, Pallas kernels, local(): pl.pallas_call(functools.partial(kernel, n, step, fam), out_shape=tuple((...  70.8 us
    pallas_call x1, Pallas kernels, local(): pl.pallas_call(unpack_kernel, out_shape=tuple((jax.ShapeDtypeStruct(shape...  2.54 us

commit v1 on v0

v1 whole, which is shorter than its diff:
```python
import functools

import jax
import jax.numpy as jnp
from jax import lax
from jax.experimental import pallas as pl
from jax.experimental.pallas import tpu as pltpu
from jax.sharding import PartitionSpec as P

F32, BF16 = jnp.float32, jnp.bfloat16
LANES = 128


def split(x):
    hi = x.astype(BF16)
    return hi, (x - hi.astype(F32)).astype(BF16)


def nn(a, b):
    return jnp.dot(a, b, preferred_element_type=F32)


def nt(a, b):
    return lax.dot_general(a, b, (((1,), (1,)), ((), ())), preferred_element_type=F32)


def remote(src, dst, send, recv, target):
    return pltpu.make_async_remote_copy(
        src_ref=src,
        dst_ref=dst,
        send_sem=send,
        recv_sem=recv,
        device_id={"row": target},
        device_id_type=pl.DeviceIdType.MESH,
    )


def each(start, stop, body):
    def one(k, _):
        body(k)
        return 0

    lax.fori_loop(start, stop, one, 0)


def sides(n):
    half, across = n // 2, 1
    while half % (2 * across) == 0 and 4 * across * across <= half:
        across *= 2
    return half // across, across


class Place:
    def __init__(self, n):
        self.n = n
        self.deep, self.wide = sides(n)
        self.me = lax.axis_index("row")
        self.core = lax.rem(self.me, 2)
        chip = lax.div(self.me, 2)
        self.x = lax.rem(chip, self.wide)
        self.z = lax.div(chip, self.wide)
        self.partner = self.at(0, 0, True)

    def at(self, k, m, other=False):
        z = lax.rem(self.z + k + self.deep, self.deep)
        x = lax.rem(self.x + m + self.wide, self.wide)
        core = 1 - self.core if other else self.core
        return (z * self.wide + x) * 2 + core

    def signal(self):
        barrier = pltpu.get_barrier_semaphore()

        def tell(target):
            pl.semaphore_signal(barrier, inc=1, device_id={"row": target}, device_id_type=pl.DeviceIdType.MESH)

        each(1, self.n, lambda k: tell(lax.rem(self.me + k, self.n)))

    def wait(self):
        pl.semaphore_wait(pltpu.get_barrier_semaphore(), self.n - 1)


class Spray:
    def __init__(self, place, own, out, send, recv):
        self.p, self.own, self.out, self.send, self.recv = place, own, out, send, recv

    def copy(self, owner, k, target):
        return remote(self.own, self.out.at[owner], self.send.at[k], self.recv.at[owner], target)

    def start(self):
        p = self.p
        each(1, p.n, lambda k: self.copy(p.me, k, lax.rem(p.me + k, p.n)).start())

    def finish(self):
        p = self.p

        def one(k):
            self.copy(lax.rem(p.me - k + p.n, p.n), k, p.partner).wait_recv()
            self.copy(p.me, k, p.partner).wait_send()

        each(1, p.n, one)


class Gather:
    def __init__(self, place, own, out, z_send, x_send, c_send, recv):
        self.p, self.own, self.out = place, own, out
        self.z_send, self.x_send, self.c_send, self.recv = z_send, x_send, c_send, recv

    def copy(self, src, owner, send, target):
        return remote(src, self.out(owner), send, self.recv.at[owner], target)

    def start(self):
        p = self.p
        each(1, p.deep, lambda k: self.copy(self.own, p.me, self.z_send.at[k], p.at(k, 0)).start())
        each(1, p.wide, lambda m: self.copy(self.own, p.me, self.x_send.at[m], p.at(0, m)).start())
        self.copy(self.own, p.me, self.c_send.at[0], p.partner).start()

    def landed(self, owner):
        self.copy(self.out(owner), owner, self.z_send.at[0], self.p.partner).wait_recv()

    def cross(self, first=1, last=None):
        p = self.p

        def one(k):
            owner = p.at(-k, 0)
            self.landed(owner)
            block = self.out(owner)
            each(1, p.wide, lambda m: self.copy(block, owner, self.x_send.at[k * p.wide + m], p.at(0, m)).start())
            self.copy(block, owner, self.c_send.at[k * p.wide], p.partner).start()

        each(first, p.deep if last is None else last, one)

    def pair(self):
        p = self.p

        def one(k):
            def two(m):
                owner = p.at(-k, -m)
                self.landed(owner)
                self.copy(self.out(owner), owner, self.c_send.at[k * p.wide + m], p.partner).start()

            each(1, p.wide, two)

        each(0, p.deep, one)

    def finish(self):
        p = self.p
        each(0, p.deep, lambda k: each(0, p.wide, lambda m: self.landed(p.at(-k, -m, True))))

        def sent(sem):
            self.copy(self.own, p.me, sem, p.partner).wait_send()

        each(1, p.deep, lambda k: sent(self.z_send.at[k]))
        each(0, p.deep, lambda k: each(1, p.wide, lambda m: sent(self.x_send.at[k * p.wide + m])))
        each(0, p.deep * p.wide, lambda i: sent(self.c_send.at[i]))


class Scatter:
    def __init__(self, place, x, near, mid, far, staged, *sems):
        self.p, self.x, self.near, self.mid, self.far, self.staged = place, x, near, mid, far, staged
        self.near_send, self.near_recv, self.mid_send, self.mid_recv, self.far_send, self.far_recv = sems

    def near_copy(self, k, m):
        p, i = self.p, k * self.p.wide + m
        return remote(
            self.x(p.at(k, m, True)), self.near.at[i], self.near_send.at[i], self.near_recv.at[i], p.partner
        )

    def mid_copy(self, k, m):
        p, i = self.p, k * self.p.wide + m
        return remote(self.staged.at[i], self.mid.at[i], self.mid_send.at[i], self.mid_recv.at[i], p.at(0, m))

    def far_copy(self, k):
        p = self.p
        return remote(
            self.staged.at[k * p.wide], self.far.at[k], self.far_send.at[k], self.far_recv.at[k], p.at(k, 0)
        )

    def over(self, first, body):
        p = self.p

        def one(i):
            k = lax.rem(i + 1, p.deep)
            each(first, p.wide, lambda m: body(k, m))

        each(0, p.deep, one)

    def start(self):
        self.over(1, lambda k, m: self.near_copy(k, m).start())
        each(0, self.p.deep, lambda k: self.near_copy(k, 0).start())

    def pair(self):
        p = self.p

        def merge(k, m):
            i = k * p.wide + m
            self.near_copy(k, m).wait_recv()
            self.staged[i] = self.x(p.at(k, m))[...] + self.near[i]

        def pass_on(k, m):
            merge(k, m)
            self.mid_copy(k, m).start()

        self.over(1, pass_on)
        each(0, p.deep, lambda k: merge(k, 0))

    def merge(self, k):
        i = k * self.p.wide

        def one(m):
            self.mid_copy(k, m).wait_recv()
            self.staged[i] = self.staged[i] + self.mid[i + m]

        each(1, self.p.wide, one)

    def cross(self, first=1, last=None):
        def pass_on(k):
            self.merge(k)
            self.far_copy(k).start()

        each(first, self.p.deep if last is None else last, pass_on)

    def finish(self):
        self.merge(0)

        def one(k):
            self.far_copy(k).wait_recv()
            self.staged[0] = self.staged[0] + self.far[k]

        each(1, self.p.deep, one)
        self.over(0, lambda k, m: self.near_copy(k, m).wait_send())
        self.over(1, lambda k, m: self.mid_copy(k, m).wait_send())
        each(1, self.p.deep, lambda k: self.far_copy(k).wait_send())


class Small:
    def __init__(self, place, x, out, near, rows, cols, send, near_recv, row_recv, col_recv, back_recv):
        self.p, self.x, self.out, self.near, self.rows, self.cols, self.send = place, x, out, near, rows, cols, send
        self.near_recv, self.row_recv, self.col_recv, self.back_recv = near_recv, row_recv, col_recv, back_recv
        self.half = near.shape[0]

    def part(self, ref, core):
        return ref.at[pl.ds(pl.multiple_of(core * self.half, 8), self.half), :]

    def near_copy(self):
        p = self.p
        return remote(self.part(self.x, 1 - p.core), self.near, self.send.at[0], self.near_recv.at[0], p.partner)

    def row_copy(self, m, source):
        p = self.p
        at = 1 + m
        return remote(self.rows.at[p.x], self.rows.at[source], self.send.at[at], self.row_recv.at[source], p.at(0, m))

    def col_copy(self, k, source):
        p = self.p
        at = 1 + p.wide + k
        return remote(self.cols.at[p.z], self.cols.at[source], self.send.at[at], self.col_recv.at[source], p.at(k, 0))

    def back_copy(self, core):
        p = self.p
        at = 1 + p.wide + p.deep
        mine, there = self.part(self.out, p.core), self.part(self.out, core)
        return remote(mine, there, self.send.at[at], self.back_recv.at[0], p.partner)

    def start(self):
        self.near_copy().start()

    def pair(self):
        p = self.p
        self.near_copy().wait_recv()
        self.rows[p.x] = self.part(self.x, p.core)[...] + self.near[...]
        each(1, p.wide, lambda m: self.row_copy(m, p.x).start())

    def across(self):
        p = self.p
        each(1, p.wide, lambda m: self.row_copy(m, lax.rem(p.x - m + p.wide, p.wide)).wait_recv())
        total = self.rows[0]
        for m in range(1, p.wide):
            total = total + self.rows[m]
        self.cols[p.z] = total
        each(1, p.deep, lambda k: self.col_copy(k, p.z).start())

    def along(self):
        p = self.p
        each(1, p.deep, lambda k: self.col_copy(k, lax.rem(p.z - k + p.deep, p.deep)).wait_recv())
        total = self.cols[0]
        for k in range(1, p.deep):
            total = total + self.cols[k]
        self.part(self.out, p.core)[...] = total
        self.back_copy(p.core).start()

    def finish(self):
        p = self.p
        self.back_copy(1 - p.core).wait_recv()
        self.near_copy().wait_send()
        each(1, p.wide, lambda m: self.row_copy(m, p.x).wait_send())
        each(1, p.deep, lambda k: self.col_copy(k, p.z).wait_send())
        self.back_copy(p.core).wait_send()


def small_scratch(n, block):
    deep, wide = sides(n)
    sems = (1 + wide + deep + 1, 1, wide, deep, 1)
    return [pltpu.VMEM(c + block, F32) for c in ((), (wide,), (deep,))] + [pltpu.SemaphoreType.DMA((c,)) for c in sems]


def gather_sems(n):
    deep, wide = sides(n)
    return [pltpu.SemaphoreType.DMA((c,)) for c in (deep, deep * wide, deep * wide, n)]


def scatter_scratch(n, block):
    deep, wide = sides(n)
    most = deep * wide
    return [pltpu.VMEM((c,) + block, F32) for c in (most, most, deep, most)] + [
        pltpu.SemaphoreType.DMA((c,)) for c in (most, most, most, most, deep, deep)
    ]


def three(dot, a, b):
    a_hi, a_lo = split(a)
    b_hi, b_lo = split(b)
    return dot(a_hi, b_hi) + dot(a_hi, b_lo) + dot(a_lo, b_hi)


def kernel(
    n,
    step,
    fam,
    act_hbm,
    valid,
    flags,
    w_left,
    w_right,
    w_hbm,
    cdd_hbm,
    align,
    total_sum,
    small_sum,
    *scratch,
):
    scratch = list(scratch)

    def take(count):
        taken = scratch[:count]
        del scratch[:count]
        return taken

    act, w_final, cdd, u_hi, u_lo, s_hi, s_lo, c_hi, c_lo, terms, terms_split = take(11)
    left, own_right, marks_all, right_all, flat_marks, turned, rt_hi, rt_lo, left_grad, both, packed, grads = take(12)
    board, marks, own_marks, factors, flat_right = take(5)
    load, mark_send, mark_recv = take(3)
    right_sems, sum_sems = take(4), take(4)
    right_scatter, sum_scatter = take(10), take(10)
    small = take(8)
    assert not scratch

    rows, total, pair = cdd.shape
    width = w_left.shape[0]
    groups = rows // step
    place = Place(n)
    place.signal()

    act_copy = pltpu.make_async_copy(act_hbm, act, load.at[groups])
    w_copy = pltpu.make_async_copy(w_hbm, w_final, load.at[groups + 1])
    act_copy.start()
    w_copy.start()

    def fetch(g):
        at = pl.ds(g * step, step)
        return pltpu.make_async_copy(cdd_hbm.at[at], cdd.at[at], load.at[g])

    each(0, groups, lambda g: fetch(g).start())

    board[...] = jnp.zeros_like(board)
    board[:fam, :rows] = valid[...].astype(F32)
    board[fam : fam + 1, :rows] = flags[...].astype(F32)
    marks[...] = board[...].T[:rows]
    keep_t = marks[:, :fam]
    lane = lax.broadcasted_iota(jnp.int32, (rows, LANES), 1)
    kept = jnp.where(lane < fam, marks[...], 0.0).astype(BF16)
    slot = 32
    tall = min(rows, 8)
    own_marks[...] = jnp.zeros_like(own_marks)
    for q in range(rows // tall):
        own_marks[:tall, q * slot : (q + 1) * slot] = marks[q * tall : (q + 1) * tall, :slot]

    w_cat = jnp.concatenate([w_left[...], w_right[...]], axis=0)
    act_copy.wait()
    projected = three(nt, act[...], w_cat)
    rights = []
    for s in range(fam):
        one = projected[s * rows : (s + 1) * rows] * keep_t[:, s : s + 1]
        rights.append(one[:, width:])
        left[pl.ds(s, rows, stride=fam), :] = jnp.concatenate([one, jnp.zeros((rows, LANES - 2 * width), F32)], axis=1)
    own_right[...] = jnp.concatenate(rights, axis=1)

    mark_spray = Spray(place, own_marks, marks_all, mark_send, mark_recv)
    right_gather = Gather(place, own_right, lambda o: right_all.at[o], *right_sems)
    place.wait()
    mark_spray.start()
    right_gather.start()
    marks_all[place.me] = own_marks[...]
    right_all[place.me] = own_right[...]
    w_copy.wait()

    def weights(q):
        parts = [w_final[pl.ds(2 * q + b, width, stride=width), :] for b in range(2)]
        return jnp.concatenate(parts, axis=1)

    l_hi, l_lo = split(left[:, :width])
    l_three = jnp.concatenate([l_hi.astype(F32), l_hi.astype(F32), l_lo.astype(F32)], axis=1).astype(BF16)

    def make_u(t):
        for half in range(2):
            q = 2 * t + half
            w_hi, w_lo = split(weights(q))
            hi, lo = split(nn(l_three, jnp.concatenate([w_hi, w_lo, w_hi], axis=0)))
            for b in range(2):
                at = pl.ds(pl.multiple_of((2 * q + b) * fam, fam), fam)
                for r in range(rows):
                    from_rows, from_lanes = slice(r * fam, (r + 1) * fam), slice(b * pair, (b + 1) * pair)
                    u_hi[at, r * pair : (r + 1) * pair] = hi[from_rows, from_lanes]
                    u_lo[at, r * pair : (r + 1) * pair] = lo[from_rows, from_lanes]

    each(0, width // 4, make_u)
    each(0, groups, lambda g: fetch(g).wait())
    mark_spray.finish()
    for o in range(n):
        block = marks_all[o]
        for q in range(rows // tall):
            turn = pltpu.roll(block, LANES - q * slot, 1) if q else block
            flat_marks[o * rows + q * tall : o * rows + (q + 1) * tall, :] = turn[:tall]
    count = nt(flat_marks[...].astype(BF16), kept)
    factors[:, :rows] = flat_marks[:, fam : fam + 1] * board[fam : fam + 1, :rows] / jnp.maximum(count, 1.0)

    def make_scaled(g):
        for r in range(g * step, (g + 1) * step):
            hi, lo = split(cdd[r] * factors[:, r : r + 1])
            s_hi[:, r * pair : (r + 1) * pair] = hi
            s_lo[:, r * pair : (r + 1) * pair] = lo

    right_gather.cross(1, 2)
    make_scaled(0)
    for g in range(groups):
        if g + 1 < groups:
            make_scaled(g + 1)
        at = slice(g * step * pair, (g + 1) * step * pair)
        value = nt(s_hi[:, at], u_hi[:, at]) + nt(s_hi[:, at], u_lo[:, at]) + nt(s_lo[:, at], u_hi[:, at])
        if g:
            value = terms[...] + value
        if g + 1 < groups:
            terms[...] = value
        else:
            for o in range(n):
                terms_split[o] = value[o * rows : (o + 1) * rows, :]
        if g == 0:
            right_gather.cross(2)
        if g == max(groups - 2, 0):
            right_gather.pair()
    right_sum = Scatter(place, lambda o: terms_split.at[o], *right_scatter)
    right_sum.start()
    right_gather.finish()

    for o in range(n):
        flat_right[o * rows : (o + 1) * rows, :] = right_all[o]
    for t in range(total // LANES):
        at = slice(t * LANES, (t + 1) * LANES)
        turned[t] = flat_right[at, :].T
        for c in range(width):
            hi, lo = split(turned[t, pl.ds(c, fam, stride=width), :])
            rt_hi[c * fam : (c + 1) * fam, at] = hi
            rt_lo[c * fam : (c + 1) * fam, at] = lo

    strip = min(4, rows) * pair
    strips = rows * pair // strip

    def make_carried(g):
        lanes = pl.ds(pl.multiple_of(g * strip, strip), strip)
        hi, lo = split(
            nn(rt_hi[...], s_hi[:, lanes]) + nn(rt_hi[...], s_lo[:, lanes]) + nn(rt_lo[...], s_hi[:, lanes])
        )
        c_hi[:, lanes] = hi
        c_lo[:, lanes] = lo

    cuts = [strips * f // 8 for f in (0, 2, 5, 7, 8)]
    deep = place.deep
    each(cuts[0], cuts[1], make_carried)
    right_sum.pair()
    for stage in range(3):
        each(cuts[stage + 1], cuts[stage + 2], make_carried)
        right_sum.cross(1 + stage * (deep - 1) // 3, 1 + (stage + 1) * (deep - 1) // 3)

    t_hi, t_lo = split(left[...].T[:width])
    t_both = jnp.concatenate([t_hi, t_lo], axis=0)

    def regroup(ref, q):
        cols = []
        for c in range(2):
            at = pl.ds(pl.multiple_of((2 * q + c) * fam, fam), fam)
            cols.append(jnp.concatenate([ref[at, r * pair : (r + 1) * pair] for r in range(rows)], axis=0))
        return jnp.concatenate(cols, axis=1)

    many = 4

    def weigh(t):
        for part in range(many):
            q = many * t + part
            two = nn(t_both, regroup(c_hi, q))
            value = two[:width] + two[width:] + nn(t_hi, regroup(c_lo, q))
            for c in range(2):
                at = pl.ds(pl.multiple_of((2 * q + c) * width, width), width)
                packed[at, :] = value[:, c * pair : (c + 1) * pair]

    each(0, width // (2 * many), weigh)

    def piece_of(ref):
        piece = ref.shape[0] // n
        return lambda o: ref.at[pl.ds(pl.multiple_of(o * piece, 8), piece), :]

    if packed.shape[0] > width * width:
        packed[width * width :, :] = jnp.zeros((packed.shape[0] - width * width, LANES), F32)
    weight_sum = Scatter(place, piece_of(packed), *sum_scatter)
    weight_sum.start()

    left_grad[...] = jnp.zeros_like(left_grad)

    def contract(t):
        qs = [many * t + part for part in range(many)]
        w_hi, w_lo = split(jnp.concatenate([weights(q) for q in qs], axis=1))
        hi = jnp.concatenate([regroup(c_hi, q) for q in qs], axis=1)
        lo = jnp.concatenate([regroup(c_lo, q) for q in qs], axis=1)
        first = jnp.concatenate([w_hi, w_lo], axis=0)
        second = jnp.concatenate([w_hi, jnp.zeros_like(w_lo)], axis=0)
        left_grad[:, : 2 * width] += nt(hi, first) + nt(lo, second)

    steps = width // (2 * many)
    each(0, steps // 2, contract)
    weight_sum.pair()
    each(steps // 2, steps, contract)
    right_sum.finish()

    mine = right_scatter[3]
    flat_right[:LANES, :] = jnp.zeros((LANES, width * fam), F32)
    flat_right[:rows, :] = mine[0]
    turned[0] = flat_right[:LANES, :].T
    per = LANES // width
    for t in range(fam // per):
        stack = [turned[0, pl.ds(per * t + c, width, stride=fam), :] for c in range(per)]
        back = jnp.concatenate(stack, axis=0).T[:rows]
        for c in range(per):
            s = per * t + c
            wide_left = left_grad[pl.ds(s, rows, stride=fam), :]
            one = jnp.concatenate(
                [wide_left[:, :width] + wide_left[:, width : 2 * width], back[:, c * width : (c + 1) * width]], axis=1
            )
            both[s * rows : (s + 1) * rows, :] = jnp.concatenate(
                [one * keep_t[:, s : s + 1], jnp.zeros((rows, LANES - 2 * width), F32)], axis=1
            )
    value = three(nn, both[...].T, act[...])[: 2 * width]
    for t in range(act.shape[1] // LANES):
        grads[t * 2 * width : (t + 1) * 2 * width, :] = value[:, t * LANES : (t + 1) * LANES]
    small_total = Small(place, grads, small_sum, *small)
    small_total.start()
    weight_sum.cross()
    small_total.pair()
    align[...] = three(nn, both[:, : 2 * width], w_cat)
    small_total.across()
    weight_sum.finish()
    summed = sum_scatter[3]
    spread = Gather(place, summed.at[0], piece_of(total_sum), *sum_sems)
    spread.start()
    piece = total_sum.shape[0] // n
    total_sum[pl.ds(pl.multiple_of(place.me * piece, 8), piece), :] = summed[0]
    small_total.along()
    spread.cross()
    spread.pair()
    small_total.finish()
    spread.finish()


def unpack_kernel(align, total_sum, small_sum, align_out, left_w, right_w, out_w):
    width, depth = left_w.shape
    align_out[...] = align[...]
    for c in range(width):
        out_w[pl.ds(c, width, stride=width), :] = total_sum[c * width : (c + 1) * width, :]
    for t in range(depth // LANES):
        at = slice(t * LANES, (t + 1) * LANES)
        first = t * 2 * width
        left_w[:, at] = small_sum[first : first + width, :]
        right_w[:, at] = small_sum[first + width : first + 2 * width, :]


def local(n, act, valid, flags, w_left, w_right, w_final, cdd):
    rows, total, pair = cdd.shape
    fam, _, depth = act.shape
    width = w_left.shape[1]
    feats = width * fam
    step = min(8, rows)
    groups = rows // step
    piece = -(-(width * width) // (8 * n)) * 8
    extra = 2 * depth * width // LANES
    vm = pl.BlockSpec(memory_space=pltpu.VMEM)
    hbm = pl.BlockSpec(memory_space=pl.ANY)
    f32 = lambda *shape: pltpu.VMEM(shape, F32)
    b16 = lambda *shape: pltpu.VMEM(shape, BF16)
    align, total_sum, small_sum = pl.pallas_call(
        functools.partial(kernel, n, step, fam),
        out_shape=tuple(
            jax.ShapeDtypeStruct(shape, F32) for shape in ((fam * rows, depth), (n * piece, LANES), (extra, LANES))
        ),
        in_specs=[hbm] + [vm] * 4 + [hbm] * 2,
        out_specs=(vm,) * 3,
        scratch_shapes=[
            f32(fam * rows, depth),
            f32(width * width, pair),
            f32(rows, total, pair),
            b16(feats, rows * pair),
            b16(feats, rows * pair),
            b16(total, rows * pair),
            b16(total, rows * pair),
            b16(feats, rows * pair),
            b16(feats, rows * pair),
            f32(total, feats),
            f32(n, rows, feats),
            f32(rows * fam, LANES),
            f32(rows, feats),
            f32(n, 8, LANES),
            f32(n, rows, feats),
            f32(total, LANES),
            f32(total // LANES, feats, LANES),
            b16(feats, total),
            b16(feats, total),
            f32(rows * fam, LANES),
            f32(fam * rows, LANES),
            f32(n * piece, LANES),
            f32(extra, LANES),
            f32(LANES, LANES),
            f32(rows, LANES),
            f32(8, LANES),
            f32(total, LANES),
            f32(total, feats),
            pltpu.SemaphoreType.DMA((groups + 2,)),
            pltpu.SemaphoreType.DMA((n,)),
            pltpu.SemaphoreType.DMA((n,)),
        ]
        + gather_sems(n) * 2
        + scatter_scratch(n, (rows, feats))
        + scatter_scratch(n, (piece, LANES))
        + small_scratch(n, (extra // 2, LANES)),
        name="outer_mean_grad",
        compiler_params=pltpu.CompilerParams(collective_id=0, has_side_effects=True, vmem_limit_bytes=60 << 20),
    )(
        act.reshape(fam * rows, depth),
        valid,
        flags.reshape(1, rows),
        w_left.T,
        w_right.T,
        w_final,
        cdd,
    )
    align, left_w, right_w, out_w = pl.pallas_call(
        unpack_kernel,
        out_shape=tuple(
            jax.ShapeDtypeStruct(shape, F32)
            for shape in ((fam * rows, depth), (width, depth), (width, depth), (width * width, pair))
        ),
        in_specs=[vm] * 3,
        out_specs=(vm,) * 4,
        name="unpack",
    )(align, total_sum, small_sum)
    return align.reshape(fam, rows, depth), left_w.T, right_w.T, out_w


def solution(mesh):
    in_specs = (
        P("groups", "row", None),
        P("groups", "row"),
        P(("groups", "row")),
        P(),
        P(),
        P(),
        P(("groups", "row"), None, None),
    )
    out_specs = (P("groups", "row", None), P("groups", None), P("groups", None), P("groups", None))
    body = functools.partial(local, mesh.shape["row"])
    return jax.shard_map(body, mesh=mesh, in_specs=in_specs, out_specs=out_specs, check_vma=False)
```

time: 74.1 us -> 60 us (0.81)
  Pallas kernels: 73.3 us -> 59.1 us
    pallas_call x1, Pallas kernels: 70.8 us -> 56.6 us  [local(): pl.pallas_call(functools.partial(kernel, n, step, fam), out_shape=tuple((...]
where the time goes in v1:
time: 60 us; the launch traced here: 59.8 us
  Pallas kernels  59.1 us (98%)
  between operations  0.64 us (1%)
    pallas_call x1, Pallas kernels, local(): pl.pallas_call(functools.partial(kernel, n, step, fam), out_shape=tuple((...  56.6 us
    pallas_call x1, Pallas kernels, local(): pl.pallas_call(unpack_kernel, out_shape=tuple((jax.ShapeDtypeStruct(shape...  2.52 us

profile of v1, /device:TPU:0, one launch (start us, length us, event | category | flops | bytes accessed | tf_op | source)
XLA Modules:
  0.0 59.8 jit_solution(468044714065034572)
XLA Ops:
  0.6 56.6 %outer_mean_grad.1 = (f32[512,256]{1,0:T(8,128)}, f32[1024,128]{1,0:T(8,128)}, f32[128,128]{1,0:T(8,128)}) custom-call(f32[512,256]{1,0:T(8,128)} %bitcast.7, s32[16,32]{1,0:T(8,128)} %valid.1, s32[1,32]{1,0:T(1,128)} %bitcast.10, f32[32,256]{1,0:T(8,128)} %bitcast.8, f32[32,256]{1,0:T(8,128)} %bitcast.9, f32[1024,128]{1,0:T(8,128)} %w_hbm.1, ...), custom_call_target="tpu_custom_call" | custom-call | tf_op jit(solution)/shard_map/outer_mean_grad/pallas_call | solution.py:606
  57.3 2.5 %unpack.1 = (f32[512,256]{1,0:T(8,128)}, f32[32,256]{1,0:T(8,128)}, f32[32,256]{1,0:T(8,128)}, f32[1024,128]{1,0:T(8,128)}) custom-call(f32[512,256]{1,0:T(8,128)} %get-tuple-element.11.align, f32[1024,128]{1,0:T(8,128)} %get-tuple-element.12.total_sum, f32[128,128]{1,0:T(8,128)} %get-tuple-element.13.small_sum), custom_call_target="tpu_custom_call" | custom-call | tf_op jit(solution)/shard_map/unpack/pallas_call | solution.py:661

commit v2 on v1

--- a/solution.py
+++ b/solution.py
@@ -78,6 +78,14 @@
     def wait(self):
         pl.semaphore_wait(pltpu.get_barrier_semaphore(), self.n - 1)
 
+    def sweep(self, distances, body):
+        for distance in distances:
+            for off in (distance, -distance):
+                there = self.z + off
+                pl.when((there >= 0) & (there < self.deep))(
+                    functools.partial(body, lax.rem(off + self.deep + self.deep, self.deep))
+                )
+
 
 class Spray:
     def __init__(self, place, own, out, send, recv):
@@ -110,7 +118,9 @@
 
     def start(self):
         p = self.p
-        each(1, p.deep, lambda k: self.copy(self.own, p.me, self.z_send.at[k], p.at(k, 0)).start())
+        p.sweep(
+            range(p.deep - 1, 0, -1), lambda k: self.copy(self.own, p.me, self.z_send.at[k], p.at(k, 0)).start()
+        )
         each(1, p.wide, lambda m: self.copy(self.own, p.me, self.x_send.at[m], p.at(0, m)).start())
         self.copy(self.own, p.me, self.c_send.at[0], p.partner).start()
 
@@ -121,26 +131,27 @@
         p = self.p
 
         def one(k):
-            owner = p.at(-k, 0)
+            owner = p.at(k, 0)
             self.landed(owner)
             block = self.out(owner)
             each(1, p.wide, lambda m: self.copy(block, owner, self.x_send.at[k * p.wide + m], p.at(0, m)).start())
             self.copy(block, owner, self.c_send.at[k * p.wide], p.partner).start()
 
-        each(first, p.deep if last is None else last, one)
+        p.sweep(range(first, p.deep if last is None else last), one)
 
     def pair(self):
         p = self.p
 
         def one(k):
             def two(m):
-                owner = p.at(-k, -m)
+                owner = p.at(k, -m)
                 self.landed(owner)
                 self.copy(self.out(owner), owner, self.c_send.at[k * p.wide + m], p.partner).start()
 
             each(1, p.wide, two)
 
-        each(0, p.deep, one)
+        one(0)
+        p.sweep(range(1, p.deep), one)
 
     def finish(self):
         p = self.p
@@ -188,20 +199,36 @@
         self.over(1, lambda k, m: self.near_copy(k, m).start())
         each(0, self.p.deep, lambda k: self.near_copy(k, 0).start())
 
+    def join(self, k, m):
+        i = k * self.p.wide + m
+        self.near_copy(k, m).wait_recv()
+        self.staged[i] = self.x(self.p.at(k, m))[...] + self.near[i]
+
+    def join_on(self, k, m):
+        self.join(k, m)
+        self.mid_copy(k, m).start()
+
     def pair(self):
-        p = self.p
-
-        def merge(k, m):
-            i = k * p.wide + m
-            self.near_copy(k, m).wait_recv()
-            self.staged[i] = self.x(p.at(k, m))[...] + self.near[i]
-
-        def pass_on(k, m):
-            merge(k, m)
-            self.mid_copy(k, m).start()
-
-        self.over(1, pass_on)
-        each(0, p.deep, lambda k: merge(k, 0))
+        self.over(1, self.join_on)
+        each(0, self.p.deep, lambda k: self.join(k, 0))
+
+    def to(self, z):
+        return lax.rem(z - self.p.z + self.p.deep, self.p.deep)
+
+    def start_to(self, z):
+        k = self.to(z)
+        each(1, self.p.wide, lambda m: self.near_copy(k, m).start())
+        self.near_copy(k, 0).start()
+
+    def pair_to(self, z):
+        k = self.to(z)
+        each(1, self.p.wide, lambda m: self.join_on(k, m))
+        self.join(k, 0)
+
+    def cross_to(self, z):
+        k = self.to(z)
+        self.merge(k)
+        pl.when(z != self.p.z)(lambda: self.far_copy(k).start())
 
     def merge(self, k):
         i = k * self.p.wide
@@ -220,8 +247,6 @@
         each(first, self.p.deep if last is None else last, pass_on)
 
     def finish(self):
-        self.merge(0)
-
         def one(k):
             self.far_copy(k).wait_recv()
             self.staged[0] = self.staged[0] + self.far[k]
@@ -334,8 +359,9 @@
     w_hbm,
     cdd_hbm,
     align,
-    total_sum,
-    small_sum,
+    left_w,
+    right_w,
+    out_w,
     *scratch,
 ):
     scratch = list(scratch)
@@ -347,7 +373,7 @@
 
     act, w_final, cdd, u_hi, u_lo, s_hi, s_lo, c_hi, c_lo, terms, terms_split = take(11)
     left, own_right, marks_all, right_all, flat_marks, turned, rt_hi, rt_lo, left_grad, both, packed, grads = take(12)
-    board, marks, own_marks, factors, flat_right = take(5)
+    board, marks, own_marks, factors, flat_right, total_sum, small_sum = take(7)
     load, mark_send, mark_recv = take(3)
     right_sems, sum_sems = take(4), take(4)
     right_scatter, sum_scatter = take(10), take(10)
@@ -357,12 +383,11 @@
     rows, total, pair = cdd.shape
     width = w_left.shape[0]
     groups = rows // step
-    place = Place(n)
-    place.signal()
-
     act_copy = pltpu.make_async_copy(act_hbm, act, load.at[groups])
     w_copy = pltpu.make_async_copy(w_hbm, w_final, load.at[groups + 1])
     act_copy.start()
+    place = Place(n)
+    place.signal()
     w_copy.start()
 
     def fetch(g):
@@ -482,7 +507,7 @@
         c_hi[:, lanes] = hi
         c_lo[:, lanes] = lo
 
-    cuts = [strips * f // 8 for f in (0, 2, 5, 7, 8)]
+    cuts = [strips * f // 8 for f in (0, 1, 5, 7, 8)]
     deep = place.deep
     each(cuts[0], cuts[1], make_carried)
     right_sum.pair()
@@ -511,16 +536,23 @@
                 at = pl.ds(pl.multiple_of((2 * q + c) * width, width), width)
                 packed[at, :] = value[:, c * pair : (c + 1) * pair]
 
-    each(0, width // (2 * many), weigh)
-
     def piece_of(ref):
         piece = ref.shape[0] // n
         return lambda o: ref.at[pl.ds(pl.multiple_of(o * piece, 8), piece), :]
 
-    if packed.shape[0] > width * width:
-        packed[width * width :, :] = jnp.zeros((packed.shape[0] - width * width, LANES), F32)
+    steps = width // (2 * many)
+
+    def planes(t):
+        return range(t * deep // steps, (t + 1) * deep // steps)
+
     weight_sum = Scatter(place, piece_of(packed), *sum_scatter)
-    weight_sum.start()
+    for t in range(steps):
+        each(t, t + 1, weigh)
+        for z in planes(t):
+            weight_sum.start_to(z)
+        if t >= 2:
+            for z in planes(t - 2):
+                weight_sum.pair_to(z)
 
     left_grad[...] = jnp.zeros_like(left_grad)
 
@@ -533,10 +565,15 @@
         second = jnp.concatenate([w_hi, jnp.zeros_like(w_lo)], axis=0)
         left_grad[:, : 2 * width] += nt(hi, first) + nt(lo, second)
 
-    steps = width // (2 * many)
-    each(0, steps // 2, contract)
-    weight_sum.pair()
-    each(steps // 2, steps, contract)
+    for t in range(steps):
+        each(t, t + 1, contract)
+        if t == 0:
+            for z in range((steps - 2) * deep // steps, deep):
+                weight_sum.pair_to(z)
+        crossed = {1: planes(0), 2: range(deep // steps, 3 * deep // steps), 3: planes(3)}
+        for z in crossed.get(t, ()):
+            weight_sum.cross_to(z)
+    right_sum.merge(0)
     right_sum.finish()
 
     mine = right_scatter[3]
@@ -561,33 +598,27 @@
         grads[t * 2 * width : (t + 1) * 2 * width, :] = value[:, t * LANES : (t + 1) * LANES]
     small_total = Small(place, grads, small_sum, *small)
     small_total.start()
-    weight_sum.cross()
+    align[...] = three(nn, both[:, : 2 * width], w_cat)
     small_total.pair()
-    align[...] = three(nn, both[:, : 2 * width], w_cat)
+    summed = sum_scatter[3]
+    spread = Gather(place, summed.at[0], piece_of(total_sum), *sum_sems)
     small_total.across()
     weight_sum.finish()
-    summed = sum_scatter[3]
-    spread = Gather(place, summed.at[0], piece_of(total_sum), *sum_sems)
     spread.start()
     piece = total_sum.shape[0] // n
     total_sum[pl.ds(pl.multiple_of(place.me * piece, 8), piece), :] = summed[0]
+    spread.cross()
     small_total.along()
-    spread.cross()
     spread.pair()
     small_total.finish()
-    spread.finish()
-
-
-def unpack_kernel(align, total_sum, small_sum, align_out, left_w, right_w, out_w):
-    width, depth = left_w.shape
-    align_out[...] = align[...]
-    for c in range(width):
-        out_w[pl.ds(c, width, stride=width), :] = total_sum[c * width : (c + 1) * width, :]
-    for t in range(depth // LANES):
+    for t in range(left_w.shape[1] // LANES):
         at = slice(t * LANES, (t + 1) * LANES)
         first = t * 2 * width
         left_w[:, at] = small_sum[first : first + width, :]
         right_w[:, at] = small_sum[first + width : first + 2 * width, :]
+    spread.finish()
+    for c in range(width):
+        out_w[pl.ds(c, width, stride=width), :] = total_sum[c * width : (c + 1) * width, :]
 
 
 def local(n, act, valid, flags, w_left, w_right, w_final, cdd):
@@ -603,13 +634,14 @@
     hbm = pl.BlockSpec(memory_space=pl.ANY)
     f32 = lambda *shape: pltpu.VMEM(shape, F32)
     b16 = lambda *shape: pltpu.VMEM(shape, BF16)
-    align, total_sum, small_sum = pl.pallas_call(
+    align, left_w, right_w, out_w = pl.pallas_call(
         functools.partial(kernel, n, step, fam),
         out_shape=tuple(
-            jax.ShapeDtypeStruct(shape, F32) for shape in ((fam * rows, depth), (n * piece, LANES), (extra, LANES))
+            pltpu.VMEM(shape, F32)
+            for shape in ((fam * rows, depth), (width, depth), (width, depth), (width * width, pair))
         ),
         in_specs=[hbm] + [vm] * 4 + [hbm] * 2,
-        out_specs=(vm,) * 3,
+        out_specs=(vm,) * 4,
         scratch_shapes=[
             f32(fam * rows, depth),
             f32(width * width, pair),
@@ -639,6 +671,8 @@
             f32(8, LANES),
             f32(total, LANES),
             f32(total, feats),
+            f32(n * piece, LANES),
+            f32(extra, LANES),
             pltpu.SemaphoreType.DMA((groups + 2,)),
             pltpu.SemaphoreType.DMA((n,)),
             pltpu.SemaphoreType.DMA((n,)),
@@ -648,7 +682,7 @@
         + scatter_scratch(n, (piece, LANES))
         + small_scratch(n, (extra // 2, LANES)),
         name="outer_mean_grad",
-        compiler_params=pltpu.CompilerParams(collective_id=0, has_side_effects=True, vmem_limit_bytes=60 << 20),
+        compiler_params=pltpu.CompilerParams(collective_id=0, has_side_effects=True, vmem_limit_bytes=58 << 20),
     )(
         act.reshape(fam * rows, depth),
         valid,
@@ -658,16 +692,6 @@
         w_final,
         cdd,
     )
-    align, left_w, right_w, out_w = pl.pallas_call(
-        unpack_kernel,
-        out_shape=tuple(
-            jax.ShapeDtypeStruct(shape, F32)
-            for shape in ((fam * rows, depth), (width, depth), (width, depth), (width * width, pair))
-        ),
-        in_specs=[vm] * 3,
-        out_specs=(vm,) * 4,
-        name="unpack",
-    )(align, total_sum, small_sum)
     return align.reshape(fam, rows, depth), left_w.T, right_w.T, out_w
 
 

time: 60 us -> 60.5 us (level)
  local copies, waits for them, and re-layouts: 0 us -> 2.82 us
  Pallas kernels: 59.1 us -> 56.8 us
    unnamed x0 -> x4, local copies, waits for them, and re-layouts: none -> 2.82 us
    pallas_call x1 -> x0, Pallas kernels: 2.52 us -> none  [local(): pl.pallas_call(unpack_kernel, out_shape=tuple((jax.ShapeDtypeStruct(shape...]
where the time goes in v2:
time: 60.5 us; the launch traced here: 60.3 us
  Pallas kernels  56.8 us (94%)
  local copies, waits for them, and re-layouts  2.82 us (5%)
  between operations  0.64 us (1%)
    pallas_call x1, Pallas kernels, local(): pl.pallas_call(functools.partial(kernel, n, step, fam), out_shape=tuple((...  56.8 us
    unnamed x4, local copies, waits for them, and re-layouts  2.82 us

profile of v2, /device:TPU:0, one launch (start us, length us, event | category | flops | bytes accessed | tf_op | source)
XLA Modules:
  0.0 60.3 jit_solution(13696547042150992015)
XLA Ops:
  0.6 56.8 %outer_mean_grad.1 = (f32[512,256]{1,0:T(8,128)S(1)}, f32[32,256]{1,0:T(8,128)S(1)}, f32[32,256]{1,0:T(8,128)S(1)}, f32[1024,128]{1,0:T(8,128)S(1)}) custom-call(f32[512,256]{1,0:T(8,128)} %bitcast.10, s32[16,32]{1,0:T(8,128)} %valid.1, s32[1,32]{1,0:T(1,128)} %bitcast.13, f32[32,256]{1,0:T(8,128)} %bitcast.11, f32[32,256]{1,0:T(8,128)} %bitcast.12, ...), custom_call_target="tpu_custom_call" | custom-call | tf_op jit(solution)/shard_map/outer_mean_grad/pallas_call | solution.py:637
  57.5 0.8 %copy.15 = f32[16,32,256]{2,1,0:T(8,128)} copy(f32[16,32,256]{2,1,0:T(8,128)S(1)} %bitcast.7) | data formatting | bytes 1048576
  58.3 0.6 %copy.16 = f32[256,32]{0,1:T(8,128)} copy(f32[256,32]{0,1:T(8,128)S(1)} %bitcast.9) | data formatting | bytes 65536
  58.9 0.6 %copy.17 = f32[256,32]{0,1:T(8,128)} copy(f32[256,32]{0,1:T(8,128)S(1)} %bitcast.8) | data formatting | bytes 65536
  59.5 0.8 %copy.18 = f32[1024,128]{1,0:T(8,128)} copy(f32[1024,128]{1,0:T(8,128)S(1)} %get-tuple-element.15) | data formatting | bytes 1048576

commit v3 on v2

--- a/solution.py
+++ b/solution.py
@@ -116,10 +116,11 @@
     def copy(self, src, owner, send, target):
         return remote(src, self.out(owner), send, self.recv.at[owner], target)
 
-    def start(self):
-        p = self.p
+    def start(self, near_first=False):
+        p = self.p
+        order = range(1, p.deep)
         p.sweep(
-            range(p.deep - 1, 0, -1), lambda k: self.copy(self.own, p.me, self.z_send.at[k], p.at(k, 0)).start()
+            order if near_first else order[::-1], lambda k: self.copy(self.own, p.me, self.z_send.at[k], p.at(k, 0)).start()
         )
         each(1, p.wide, lambda m: self.copy(self.own, p.me, self.x_send.at[m], p.at(0, m)).start())
         self.copy(self.own, p.me, self.c_send.at[0], p.partner).start()
@@ -258,33 +259,46 @@
 
 
 class Small:
-    def __init__(self, place, x, out, near, rows, cols, send, near_recv, row_recv, col_recv, back_recv):
-        self.p, self.x, self.out, self.near, self.rows, self.cols, self.send = place, x, out, near, rows, cols, send
-        self.near_recv, self.row_recv, self.col_recv, self.back_recv = near_recv, row_recv, col_recv, back_recv
-        self.half = near.shape[0]
-
-    def part(self, ref, core):
+    def __init__(self, place, x, out, near, own, rows, cols, send, near_recv, row_recv, col_recv, slot_recv, back_recv):
+        self.p, self.x, self.out, self.near, self.own, self.rows, self.cols = place, x, out, near, own, rows, cols
+        self.near_recv, self.row_recv, self.col_recv = near_recv, row_recv, col_recv
+        self.send, self.slot_recv, self.back_recv = send, slot_recv, back_recv
+        self.half, self.part = near.shape[0], cols.shape[1]
+
+    def side(self, ref, core):
         return ref.at[pl.ds(pl.multiple_of(core * self.half, 8), self.half), :]
 
+    def slot(self, x):
+        at = self.p.core * self.half + x * self.part
+        return self.out.at[pl.ds(pl.multiple_of(at, 8), self.part), :]
+
+    def own_part(self, x):
+        return self.own.at[pl.ds(pl.multiple_of(x * self.part, 8), self.part), :]
+
     def near_copy(self):
         p = self.p
-        return remote(self.part(self.x, 1 - p.core), self.near, self.send.at[0], self.near_recv.at[0], p.partner)
+        return remote(self.side(self.x, 1 - p.core), self.near, self.send.at[0], self.near_recv.at[0], p.partner)
 
     def row_copy(self, m, source):
         p = self.p
-        at = 1 + m
-        return remote(self.rows.at[p.x], self.rows.at[source], self.send.at[at], self.row_recv.at[source], p.at(0, m))
+        src, dst = self.own_part(lax.rem(p.x + m, p.wide)), self.rows.at[source]
+        return remote(src, dst, self.send.at[1 + m], self.row_recv.at[source], p.at(0, m))
 
     def col_copy(self, k, source):
         p = self.p
         at = 1 + p.wide + k
         return remote(self.cols.at[p.z], self.cols.at[source], self.send.at[at], self.col_recv.at[source], p.at(k, 0))
 
+    def slot_copy(self, m, source):
+        p = self.p
+        at = 1 + p.wide + p.deep + m
+        return remote(self.slot(source), self.slot(source), self.send.at[at], self.slot_recv.at[source], p.at(0, m))
+
     def back_copy(self, core):
         p = self.p
-        at = 1 + p.wide + p.deep
-        mine, there = self.part(self.out, p.core), self.part(self.out, core)
-        return remote(mine, there, self.send.at[at], self.back_recv.at[0], p.partner)
+        at = 1 + p.wide + p.deep + p.wide
+        half = self.side(self.out, core)
+        return remote(half, half, self.send.at[at], self.back_recv.at[0], p.partner)
 
     def start(self):
         self.near_copy().start()
@@ -292,8 +306,9 @@
     def pair(self):
         p = self.p
         self.near_copy().wait_recv()
-        self.rows[p.x] = self.part(self.x, p.core)[...] + self.near[...]
+        self.own[...] = self.side(self.x, p.core)[...] + self.near[...]
         each(1, p.wide, lambda m: self.row_copy(m, p.x).start())
+        self.rows[p.x] = self.own_part(p.x)[...]
 
     def across(self):
         p = self.p
@@ -310,7 +325,12 @@
         total = self.cols[0]
         for k in range(1, p.deep):
             total = total + self.cols[k]
-        self.part(self.out, p.core)[...] = total
+        self.slot(p.x)[...] = total
+        each(1, p.wide, lambda m: self.slot_copy(m, p.x).start())
+
+    def back(self):
+        p = self.p
+        each(1, p.wide, lambda m: self.slot_copy(m, lax.rem(p.x - m + p.wide, p.wide)).wait_recv())
         self.back_copy(p.core).start()
 
     def finish(self):
@@ -319,13 +339,16 @@
         self.near_copy().wait_send()
         each(1, p.wide, lambda m: self.row_copy(m, p.x).wait_send())
         each(1, p.deep, lambda k: self.col_copy(k, p.z).wait_send())
+        each(1, p.wide, lambda m: self.slot_copy(m, p.x).wait_send())
         self.back_copy(p.core).wait_send()
 
 
-def small_scratch(n, block):
+def small_scratch(n, half):
     deep, wide = sides(n)
-    sems = (1 + wide + deep + 1, 1, wide, deep, 1)
-    return [pltpu.VMEM(c + block, F32) for c in ((), (wide,), (deep,))] + [pltpu.SemaphoreType.DMA((c,)) for c in sems]
+    part = half // wide
+    shapes = ((half, LANES), (half, LANES), (wide, part, LANES), (deep, part, LANES))
+    sems = (2 + wide + deep + wide, 1, wide, deep, wide, 1)
+    return [pltpu.VMEM(shape, F32) for shape in shapes] + [pltpu.SemaphoreType.DMA((c,)) for c in sems]
 
 
 def gather_sems(n):
@@ -377,7 +400,7 @@
     load, mark_send, mark_recv = take(3)
     right_sems, sum_sems = take(4), take(4)
     right_scatter, sum_scatter = take(10), take(10)
-    small = take(8)
+    small = take(10)
     assert not scratch
 
     rows, total, pair = cdd.shape
@@ -423,7 +446,6 @@
     right_gather = Gather(place, own_right, lambda o: right_all.at[o], *right_sems)
     place.wait()
     mark_spray.start()
-    right_gather.start()
     marks_all[place.me] = own_marks[...]
     right_all[place.me] = own_right[...]
     w_copy.wait()
@@ -447,7 +469,9 @@
                     u_hi[at, r * pair : (r + 1) * pair] = hi[from_rows, from_lanes]
                     u_lo[at, r * pair : (r + 1) * pair] = lo[from_rows, from_lanes]
 
-    each(0, width // 4, make_u)
+    each(0, width // 8, make_u)
+    right_gather.start(near_first=True)
+    each(width // 8, width // 4, make_u)
     each(0, groups, lambda g: fetch(g).wait())
     mark_spray.finish()
     for o in range(n):
@@ -464,8 +488,8 @@
             s_hi[:, r * pair : (r + 1) * pair] = hi
             s_lo[:, r * pair : (r + 1) * pair] = lo
 
+    make_scaled(0)
     right_gather.cross(1, 2)
-    make_scaled(0)
     for g in range(groups):
         if g + 1 < groups:
             make_scaled(g + 1)
@@ -602,14 +626,15 @@
     small_total.pair()
     summed = sum_scatter[3]
     spread = Gather(place, summed.at[0], piece_of(total_sum), *sum_sems)
-    small_total.across()
     weight_sum.finish()
     spread.start()
+    small_total.across()
     piece = total_sum.shape[0] // n
     total_sum[pl.ds(pl.multiple_of(place.me * piece, 8), piece), :] = summed[0]
     spread.cross()
     small_total.along()
     spread.pair()
+    small_total.back()
     small_total.finish()
     for t in range(left_w.shape[1] // LANES):
         at = slice(t * LANES, (t + 1) * LANES)
@@ -619,6 +644,15 @@
     spread.finish()
     for c in range(width):
         out_w[pl.ds(c, width, stride=width), :] = total_sum[c * width : (c + 1) * width, :]
+
+
+def put(*refs):
+    srcs, dsts, sems = refs[:4], refs[4:8], refs[8]
+    copies = [pltpu.make_async_copy(src, dst, sems.at[i]) for i, (src, dst) in enumerate(zip(srcs, dsts))]
+    for copy in copies:
+        copy.start()
+    for copy in copies:
+        copy.wait()
 
 
 def local(n, act, valid, flags, w_left, w_right, w_final, cdd):
@@ -680,7 +714,7 @@
         + gather_sems(n) * 2
         + scatter_scratch(n, (rows, feats))
         + scatter_scratch(n, (piece, LANES))
-        + small_scratch(n, (extra // 2, LANES)),
+        + small_scratch(n, extra // 2),
         name="outer_mean_grad",
         compiler_params=pltpu.CompilerParams(collective_id=0, has_side_effects=True, vmem_limit_bytes=58 << 20),
     )(
@@ -692,6 +726,15 @@
         w_final,
         cdd,
     )
+    align, left_w, right_w, out_w = pl.pallas_call(
+        put,
+        out_shape=tuple(jax.ShapeDtypeStruct(one.shape, F32) for one in (align, left_w, right_w, out_w)),
+        in_specs=[hbm] * 4,
+        out_specs=(hbm,) * 4,
+        scratch_shapes=[pltpu.SemaphoreType.DMA((4,))],
+        name="put",
+        compiler_params=pltpu.CompilerParams(vmem_limit_bytes=1 << 20),
+    )(align, left_w, right_w, out_w)
     return align.reshape(fam, rows, depth), left_w.T, right_w.T, out_w
 
 

time: 60.5 us -> 55.9 us (0.924)
  local copies, waits for them, and re-layouts: 2.82 us -> 0 us
  Pallas kernels: 56.8 us -> 54.9 us
    pallas_call x1, Pallas kernels: 56.8 us -> 53.9 us  [local(): pl.pallas_call(functools.partial(kernel, n, step, fam), out_shape=tuple((...]
    unnamed x4 -> x0, local copies, waits for them, and re-layouts: 2.82 us -> none
    pallas_call x0 -> x1, Pallas kernels: none -> 1.03 us  [local(): pl.pallas_call(put, out_shape=tuple((jax.ShapeDtypeStruct(one.shape, F32)...]
where the time goes in v3:
time: 55.9 us; the launch traced here: 55.7 us
  Pallas kernels  54.9 us (98%)
  between operations  0.8 us (1%)
    pallas_call x1, Pallas kernels, local(): pl.pallas_call(functools.partial(kernel, n, step, fam), out_shape=tuple((...  53.9 us

profile of v3, /device:TPU:0, one launch (start us, length us, event | category | flops | bytes accessed | tf_op | source)
XLA Modules:
  0.0 55.7 jit_solution(4217237841147515522)
XLA Ops:
  0.6 53.9 %outer_mean_grad.1 = (f32[512,256]{1,0:T(8,128)S(1)}, f32[32,256]{1,0:T(8,128)S(1)}, f32[32,256]{1,0:T(8,128)S(1)}, f32[1024,128]{1,0:T(8,128)S(1)}) custom-call(f32[512,256]{1,0:T(8,128)} %bitcast.7, s32[16,32]{1,0:T(8,128)} %valid.1, s32[1,32]{1,0:T(1,128)} %bitcast.10, f32[32,256]{1,0:T(8,128)} %bitcast.8, f32[32,256]{1,0:T(8,128)} %bitcast.9, ...), custom_call_target="tpu_custom_call" | custom-call | tf_op jit(solution)/shard_map/outer_mean_grad/pallas_call | solution.py:671
  54.5 1.0 %put.1 = (f32[512,256]{1,0:T(8,128)}, f32[32,256]{1,0:T(8,128)}, f32[32,256]{1,0:T(8,128)}, f32[1024,128]{1,0:T(8,128)}) custom-call(f32[512,256]{1,0:T(8,128)S(1)} %get-tuple-element.12.refs_0_, f32[32,256]{1,0:T(8,128)S(1)} %get-tuple-element.13.refs_1_, f32[32,256]{1,0:T(8,128)S(1)} %get-tuple-element.14.refs_2_, f32[1024,128]{1,0:T(8,128)S(1)} %get-tuple-element.15.refs_3_), custom_call_target="tpu_custom_call" | custom-call | tf_op jit(solution)/shard_map/put/pallas_call | solution.py:729
